TPU v7x, 512 devices: a whole 4x8x8 slice. The times are simulated.
512 devices in a mesh: wide: 64 (over x, y, core), narrow: 8 (over z).
Axes of the slice: x: 4, y: 8, z: 8, core: 2. Of those that a mesh axis runs over, the one named last changes fastest.
Arguments:
- points: bfloat16 [128, 1024, 512], P('wide', 'narrow'), may hold values from -6 to 6
- counts: int32 [128, 256], P('wide', 'narrow'), may hold values from 1 to 4, as said below
- destination: int32 [128, 256], P('wide', 'narrow'), may hold values from 0 to 63, as said below
- rotated_ball: int32 [128, 256], P('wide', 'narrow'), may hold values from 0 to 1
- qkv_first: bfloat16 [512, 1536], replicated, may hold values from -1 to 1
- out_first: bfloat16 [512, 512], replicated, may hold values from -0.25 to 0.25
- qkv_second: bfloat16 [512, 1536], replicated, may hold values from -1 to 1
- out_second: bfloat16 [512, 512], replicated, may hold values from -0.25 to 0.25
Outputs:
- result: bfloat16 [128, 1024, 512], P('wide', 'narrow')
Inputs may be any that keep to these rules, and one draw needn't show every extreme that they name: `counts`: the first block of every ball row has all 4 points usable. Among the blocks of one device, at most 2 have the same destination; on every device some destination receives 2 of its blocks, and some destination receives 2 blocks from every device of its narrow index.
All inputs are finite; a program needn't handle non-finite values.
Results may differ from a plain program's by a relative error of at most 0.0095.
Values may be sent and summed in bfloat16 or wider, within the bound.
A program may use at most 64 MiB of HBM per device.

v0:
```python
import math
import jax
import jax.numpy as jnp
from jax import lax
from jax.sharding import PartitionSpec as P

HEADS = 8
BLK = 4
EPSILON = 1e-06
NEGATIVE = -1e30


def rms_round(values):
    widened = values.astype(jnp.float32)
    scaled = widened * lax.rsqrt(jnp.mean(widened * widened, axis=-1, keepdims=True) + EPSILON)
    return scaled.astype(jnp.bfloat16)


def project(normed, weight):
    flat = normed.reshape(-1, normed.shape[-1])
    product = jnp.dot(flat, weight, preferred_element_type=jnp.float32)
    return product.reshape(normed.shape[:-1] + (weight.shape[1],))


def split_heads(block_rows, offset, model_width):
    head_dim = model_width // HEADS
    return block_rows[..., offset : offset + model_width].reshape(
        block_rows.shape[:-1] + (HEADS, head_dim)
    )


def usable_points(counts):
    position = lax.broadcasted_iota(jnp.int32, counts.shape + (BLK,), len(counts.shape))
    usable = position < counts[..., None]
    return usable.reshape(counts.shape[:-1] + (counts.shape[-1] * BLK,))


def pool_rows(qkv_all, counts):
    model_width = qkv_all.shape[-1] // 3
    usable = usable_points(counts)
    kv_part = qkv_all[..., model_width:].astype(jnp.float32) * usable[..., None].astype(jnp.float32)
    grouped = kv_part.reshape(counts.shape + (BLK, 2 * model_width)).sum(axis=-2)
    return (grouped / counts[..., None].astype(jnp.float32)).astype(jnp.bfloat16)


def fine_coarse(ball_qkv, fine_usable, coarse_kv):
    model_width = coarse_kv.shape[-1] // 2
    scaling = 1.0 / math.sqrt(model_width // HEADS)
    queries = split_heads(ball_qkv, 0, model_width)
    key_fine = split_heads(ball_qkv, model_width, model_width)
    value_fine = split_heads(ball_qkv, 2 * model_width, model_width)
    key_coarse = split_heads(coarse_kv, 0, model_width)
    value_coarse = split_heads(coarse_kv, model_width, model_width)
    score_fine = (
        jnp.einsum("qhe,khe->hqk", queries, key_fine, preferred_element_type=jnp.float32) * scaling
    )
    score_fine = jnp.where(fine_usable[None, None, :], score_fine, NEGATIVE)
    score_coarse = (
        jnp.einsum("qhe,khe->hqk", queries, key_coarse, preferred_element_type=jnp.float32)
        * scaling
    )
    highest = jnp.maximum(jnp.max(score_fine, axis=-1), jnp.max(score_coarse, axis=-1))[..., None]
    exp_fine = jnp.exp(score_fine - highest)
    exp_coarse = jnp.exp(score_coarse - highest)
    denominator = jnp.sum(exp_fine, axis=-1, keepdims=True) + jnp.sum(
        exp_coarse, axis=-1, keepdims=True
    )
    weight_fine = (exp_fine / denominator).astype(jnp.bfloat16)
    weight_coarse = (exp_coarse / denominator).astype(jnp.bfloat16)
    mixture = jnp.einsum(
        "hqk,khe->qhe", weight_fine, value_fine, preferred_element_type=jnp.float32
    )
    mixture = mixture + jnp.einsum(
        "hqk,khe->qhe", weight_coarse, value_coarse, preferred_element_type=jnp.float32
    )
    return mixture.reshape(mixture.shape[0], model_width).astype(jnp.bfloat16)


def ball_attention(recv_rows, row_ball, row_usable):
    total_rows = recv_rows.shape[0]
    model_width = recv_rows.shape[1] // 3
    scaling = 1.0 / math.sqrt(model_width // HEADS)
    queries = split_heads(recv_rows, 0, model_width)
    key_rows = split_heads(recv_rows, model_width, model_width)
    value_rows = split_heads(recv_rows, 2 * model_width, model_width)
    block_len = min(256, total_rows)

    def one_block(block_idx):
        offset = block_idx * block_len
        query_block = lax.dynamic_slice_in_dim(queries, offset, block_len, 0)
        ball_block = lax.dynamic_slice_in_dim(row_ball, offset, block_len, 0)
        scores = (
            jnp.einsum("qhe,khe->hqk", query_block, key_rows, preferred_element_type=jnp.float32)
            * scaling
        )
        allowed = (ball_block[:, None] == row_ball[None, :]) & row_usable[None, :]
        scores = jnp.where(allowed[None], scores, NEGATIVE)
        highest = jnp.max(scores, axis=-1, keepdims=True)
        exponent = jnp.exp(scores - highest)
        weights = (exponent / jnp.sum(exponent, axis=-1, keepdims=True)).astype(jnp.bfloat16)
        mixture = jnp.einsum(
            "hqk,khe->qhe", weights, value_rows, preferred_element_type=jnp.float32
        )
        return mixture.reshape(block_len, model_width).astype(jnp.bfloat16)

    blocks_out = lax.map(one_block, jnp.arange(total_rows // block_len, dtype=jnp.int32))
    return blocks_out.reshape(total_rows, model_width)


def on_device(
    points, counts, destination, rotated_ball, qkv_first, out_first, qkv_second, out_second
):
    model_width = points.shape[-1]
    normed_one = rms_round(points)
    qkv_one = project(normed_one, qkv_first).astype(jnp.bfloat16)
    pooled = pool_rows(qkv_one, counts)
    usable = usable_points(counts)
    pooled_all = lax.all_gather(pooled, "narrow", axis=1, tiled=True)
    attended_one = jax.vmap(fine_coarse)(qkv_one, usable, pooled_all)
    layer_one = (points.astype(jnp.float32) + project(attended_one, out_first)).astype(jnp.bfloat16)
    normed_two = rms_round(layer_one)
    wide_count = lax.axis_size("wide")
    block_count = destination.size
    capacity = max(2, 2 * block_count // wide_count)
    dest_flat = destination.reshape(block_count)
    ball_flat = rotated_ball.reshape(block_count)
    fill_flat = counts.reshape(block_count)
    onehot = (dest_flat[:, None] == jnp.arange(wide_count, dtype=jnp.int32)[None, :]).astype(
        jnp.int32
    )
    earlier = jnp.cumsum(onehot, axis=0, dtype=jnp.int32) - onehot
    rank_in = jnp.sum(earlier * onehot, axis=1, dtype=jnp.int32)
    slot_of = dest_flat * capacity + rank_in

    def packed(block_data, filler):
        buffer = jnp.full((wide_count * capacity,) + block_data.shape[1:], filler, block_data.dtype)
        return (
            buffer.at[slot_of]
            .set(block_data)
            .reshape((wide_count, capacity) + block_data.shape[1:])
        )

    ball_packed = packed(ball_flat, -1)
    fill_packed = packed(fill_flat, 0)
    qkv_two = project(normed_two, qkv_second).astype(jnp.bfloat16)
    qkv_blocks = qkv_two.reshape(block_count, BLK, 3 * model_width)
    arrived, ball_in, fill_in = (
        lax.all_to_all(packed(qkv_blocks, 0), "wide", split_axis=0, concat_axis=0, tiled=True),
        lax.all_to_all(ball_packed, "wide", split_axis=0, concat_axis=0, tiled=True),
        lax.all_to_all(fill_packed, "wide", split_axis=0, concat_axis=0, tiled=True),
    )
    recv_rows = arrived.reshape(-1, 3 * model_width)
    row_ball = jnp.broadcast_to(ball_in[..., None], ball_in.shape + (BLK,)).reshape(-1)
    row_usable = usable_points(fill_in).reshape(-1)
    mixture = ball_attention(recv_rows, row_ball, row_usable)
    returned = lax.all_to_all(
        mixture.reshape(wide_count, capacity, BLK, model_width),
        "wide",
        split_axis=0,
        concat_axis=0,
        tiled=True,
    )
    attended_two = returned.reshape(wide_count * capacity, BLK, model_width)[slot_of].reshape(
        points.shape
    )
    return (layer_one.astype(jnp.float32) + project(attended_two, out_second)).astype(jnp.bfloat16)


def solution(mesh):
    in_specs = (
        P("wide", "narrow", None),
        P("wide", "narrow"),
        P("wide", "narrow"),
        P("wide", "narrow"),
        P(),
        P(),
        P(),
        P(),
    )
    out_specs = P("wide", "narrow", None)
    return jax.shard_map(
        on_device, mesh=mesh, in_specs=in_specs, out_specs=out_specs, check_vma=False
    )
```

profile of v0, /device:TPU:1, one launch (start us, length us, event | category | flops | bytes accessed | tf_op | source)
XLA Modules:
  0.0 210.0 jit_solution(17064649044195788203)
XLA Ops:
  6.5 1.2 fusion.35
  7.8 0.7 convert_element_type.88
  8.4 0.7 lt.53
  9.4 1.6 convolution_convert_fusion.1
  11.0 1.1 convert_multiply_fusion
  12.1 1.6 reshape.243
  13.7 1.4 reduce_sum.66
  15.1 1.0 divide_convert_fusion.8
  16.1 0.8 copy.51
  17.3 0.2 select_reduce_fusion
  17.5 0.8 scatter_custom_fusion
  18.3 0.7 all_to_all.18
  19.1 11.6 %all-to-all-start = ((s32[64,1,2]{2,1,0:T(1,128)}), s32[64,1,2]{2,1,0:T(1,128)S(1)}, u32[]{:S(2)}, u32[]{:S(2)}) async-start(s32[64,1,2]{2,1,0:T(1,128)} %bitcast.11), calls=%async_computation | async-start | bytes 65536 | tf_op jit(solution)/shard_map/all_to_all | solution.py:149
  30.8 0.2 copy.49
  30.9 0.2 copy.50
  31.1 0.8 copy.48
  32.0 0.4 fusion.59
  32.3 27.9 %all-gather.2.cloned.1.call-done = bf16[2,256,1024]{2,0,1:T(2,128)(2,1)} async-done(((bf16[2,32,1024]{2,0,1:T(2,128)(2,1)}), bf16[2,256,1024]{2,0,1:T(2,128)(2,1)}) %all-gather.2.cloned.1.call-update) | async-done | bytes 1048592 | tf_op jit(solution)/shard_map/all_gather | solution.py:118
  60.2 2.7 %fusion.57 = (bf16[2,256,512]{2,0,1:T(2,128)(2,1)S(1)}, bf16[2,256,512]{2,0,1:T(2,128)(2,1)}) fusion(bf16[2,256,1024]{2,0,1:T(2,128)(2,1)} %all-gather.2.cloned.1.call-done), kind=kLoop, calls=%fused_computation.79 | loop fusion | bytes 2097152 | tf_op jit(solution)/shard_map/vmap()/slice | solution.py:27
  63.0 2.0 copy.52
  65.0 1.6 multiply_reduce_fusion
  66.6 0.2 fusion.34
  66.8 1.2 copy-done.1
  67.9 0.7 fusion.26
  68.7 1.2 copy.54
  69.9 0.3 fusion.39
  70.2 1.3 copy-done.2
  71.6 1.1 fusion.30
  72.7 0.4 multiply_reduce_fusion.1
  73.1 0.8 copy-done.3
  73.9 0.2 copy-done.6
  74.1 0.6 convolution_convert_fusion
  74.7 0.2 reshape.284
  74.9 1.6 broadcast_in_dim.71
  76.4 8.1 %scatter_fusion = bf16[128,4,1536]{2,1,0:T(4,128)(2,1)} fusion(bf16[128,4,1536]{2,1,0:T(4,128)(2,1)} %broadcast_in_dim.71, s32[64]{0:T(128)S(1)} %fusion.44, bf16[64,4,1536]{2,1,0:T(4,128)(2,1)S(1)} %reshape.284), kind=kCustom, calls=%fused_computation.3 | custom fusion | bytes 2359552 | tf_op jit(solution)/shard_map/scatter | solution.py:139
  84.5 15.0 %all-to-all-start.2 = ((bf16[64,2,4,1536]{3,2,1,0:T(4,128)(2,1)}), bf16[64,2,4,1536]{3,2,1,0:T(4,128)(2,1)S(1)}, u32[]{:S(2)}, u32[]{:S(2)}) async-start(bf16[64,2,4,1536]{3,2,1,0:T(4,128)(2,1)} %bitcast.14), calls=%async_computation.2 | async-start | bytes 3145728 | tf_op jit(solution)/shard_map/all_to_all | solution.py:148
  99.6 0.8 scatter_custom_fusion.1
  100.4 0.8 all_to_all.20
  101.6 37.7 %all-to-all-done.2 = bf16[64,2,4,1536]{3,2,1,0:T(4,128)(2,1)S(1)} async-done(((bf16[64,2,4,1536]{3,2,1,0:T(4,128)(2,1)}), bf16[64,2,4,1536]{3,2,1,0:T(4,128)(2,1)S(1)}, u32[]{:S(2)}, u32[]{:S(2)}) %all-to-all-start.2) | async-done | bytes 1572896 | tf_op jit(solution)/shard_map/all_to_all | solution.py:148
  139.3 6.1 %all-to-all-start.1 = ((s32[64,1,2]{2,1,0:T(1,128)}), s32[64,1,2]{2,1,0:T(1,128)S(1)}, u32[]{:S(2)}, u32[]{:S(2)}) async-start(s32[64,1,2]{2,1,0:T(1,128)} %bitcast.18), calls=%async_computation.1 | async-start | bytes 65536 | tf_op jit(solution)/shard_map/all_to_all | solution.py:150
  145.5 1.4 reshape.251
  146.8 1.5 fusion.56
  148.3 1.0 copy.59
  149.3 1.0 copy.60
  150.3 0.2 copy.61
  150.5 4.1 %all-to-all-done.1 = s32[64,1,2]{2,1,0:T(1,128)S(1)} async-done(((s32[64,1,2]{2,1,0:T(1,128)}), s32[64,1,2]{2,1,0:T(1,128)S(1)}, u32[]{:S(2)}, u32[]{:S(2)}) %all-to-all-start.1) | async-done | bytes 544 | tf_op jit(solution)/shard_map/all_to_all | solution.py:150
  154.7 20.9 %while.11 = (s32[]{:T(128)}, bf16[2,256,512]{2,1,0:T(8,128)(2,1)}, s32[2]{0:T(128)S(1)}, s32[512]{0:T(512)S(1)}, bf16[512,8,64]{0,2,1:T(8,128)(2,1)S(1)}, /*inde...) while((s32[]{:T(128)}, bf16[2,256,512]{2,1,0:T(8,128)(2,1)}, ...), condition=%wide.region_15.16_spmd.clone, body=%wide.region_12.15_spmd.clone.sunk | while | flops 275121152 | bytes 11303615 | solution.py:106
  154.7 0.6 dynamic_slice.29
  156.5 0.2 compare_and_fusion.2
  156.7 4.5 %fusion.79 = (f32[8,256]{1,0:T(8,128)S(1)}, f32[8,256,512]{2,1,0:T(8,128)}) fusion(pred[256,512]{1,0:T(8,128)(4,1)S(1)} %compare_and_fusion.2, bf16[512,8,64]{0,2,1:T(8,128)(2,1)} %get-tuple-element.229, bf16[512,8,64]{0,2,1:T(8,128)(2,1)S(1)} %get-tuple-element.228, s32[]{:T(128)S(6)} %select_n.46), kind=kOutput, calls=%fused_computation.77.clone.1 | convolution fusion | flops 138412544 | bytes 5120004 | tf_op jit(solution)/shard_map/while/body/eval_jaxpr/sub | solution.py:99
  161.2 3.0 %fusion.80 = bf16[8,256,64]{1,2,0:T(8,128)(2,1)S(1)} fusion(bf16[512,8,64]{0,2,1:T(8,128)(2,1)S(1)} %get-tuple-element.230, f32[8,256,512]{2,1,0:T(8,128)} %get-tuple-element.196, f32[8,256]{1,0:T(8,128)S(1)} %get-tuple-element.197), kind=kOutput, calls=%fused_computation.15.clone.1 | convolution fusion | flops 136445952 | bytes 4988928 | tf_op jit(solution)/shard_map/while/body/eval_jaxpr/hqk,khe->qhe/dot_general | solution.py:101
  164.2 0.1 copy.73
  164.4 0.7 constant_dynamic-update-slice_fusion.2
  165.1 0.6 dynamic_slice.29
  167.0 0.2 compare_and_fusion.2
  167.1 4.5 %fusion.79 = (f32[8,256]{1,0:T(8,128)S(1)}, f32[8,256,512]{2,1,0:T(8,128)}) fusion(pred[256,512]{1,0:T(8,128)(4,1)S(1)} %compare_and_fusion.2, bf16[512,8,64]{0,2,1:T(8,128)(2,1)} %get-tuple-element.229, bf16[512,8,64]{0,2,1:T(8,128)(2,1)S(1)} %get-tuple-element.228, s32[]{:T(128)S(6)} %select_n.46), kind=kOutput, calls=%fused_computation.77.clone.1 | convolution fusion | flops 138412544 | bytes 5120004 | tf_op jit(solution)/shard_map/while/body/eval_jaxpr/sub | solution.py:99
  171.7 3.0 %fusion.80 = bf16[8,256,64]{1,2,0:T(8,128)(2,1)S(1)} fusion(bf16[512,8,64]{0,2,1:T(8,128)(2,1)S(1)} %get-tuple-element.230, f32[8,256,512]{2,1,0:T(8,128)} %get-tuple-element.196, f32[8,256]{1,0:T(8,128)S(1)} %get-tuple-element.197), kind=kOutput, calls=%fused_computation.15.clone.1 | convolution fusion | flops 136445952 | bytes 4988928 | tf_op jit(solution)/shard_map/while/body/eval_jaxpr/hqk,khe->qhe/dot_general | solution.py:101
  174.7 0.1 copy.73
  174.9 0.7 constant_dynamic-update-slice_fusion.2
  175.6 2.1 reshape_reshape.4
  177.7 6.2 %all-to-all-start.3 = ((bf16[64,2,4,512]{3,2,1,0:T(4,128)(2,1)}), bf16[64,2,4,512]{3,2,1,0:T(4,128)(2,1)S(1)}, u32[]{:S(2)}, u32[]{:S(2)}) async-start(bf16[64,2,4,512]{3,2,1,0:T(4,128)(2,1)} %reshape_reshape.4), calls=%async_computation.3 | async-start | bytes 1048576 | tf_op jit(solution)/shard_map/all_to_all | solution.py:156
  183.9 17.3 %all-to-all-done.3 = bf16[64,2,4,512]{3,2,1,0:T(4,128)(2,1)S(1)} async-done(((bf16[64,2,4,512]{3,2,1,0:T(4,128)(2,1)}), bf16[64,2,4,512]{3,2,1,0:T(4,128)(2,1)S(1)}, u32[]{:S(2)}, u32[]{:S(2)}) %all-to-all-start.3) | async-done | bytes 524320 | tf_op jit(solution)/shard_map/all_to_all | solution.py:156
  201.2 0.8 gather_fusion
  202.1 1.0 fusion.33
  (64 shorter events, 2.7 us)
Async XLA Ops:
  6.5 2.9 %copy-start = (bf16[512,1536]{1,0:T(8,128)(2,1)S(1)}, bf16[512,1536]{1,0:T(8,128)(2,1)}, u32[]{:S(2)}) copy-start(bf16[512,1536]{1,0:T(8,128)(2,1)} %param.14) | copy-start | bytes 4718596
  6.5 53.7 %all-gather.2.cloned.1.call-start = ((), (), s32[]{:S(2)}) async-start(), calls=%async_computation.4 | async-start | bytes 1179648 | tf_op jit(solution)/shard_map/all_gather | solution.py:118
  12.1 4.8 %copy-start.13 = (s32[2,32]{1,0:T(2,128)S(1)}, s32[2,32]{1,0:T(2,128)}, u32[]{:S(2)}) copy-start(s32[2,32]{1,0:T(2,128)} %param.12) | copy-start | bytes 772
  12.1 5.0 %copy-start.14 = (s32[2,32]{1,0:T(2,128)S(1)}, s32[2,32]{1,0:T(2,128)}, u32[]{:S(2)}) copy-start(s32[2,32]{1,0:T(2,128)} %param.13) | copy-start | bytes 772
  19.1 65.5 %all-to-all-start = ((s32[64,1,2]{2,1,0:T(1,128)}), s32[64,1,2]{2,1,0:T(1,128)S(1)}, u32[]{:S(2)}, u32[]{:S(2)}) async-start(s32[64,1,2]{2,1,0:T(1,128)} %bitcast.11), calls=%async_computation | async-start | bytes 65536 | tf_op jit(solution)/shard_map/all_to_all | solution.py:149
  66.6 1.4 copy-start.1
  66.6 3.3 %copy-start.11 = (bf16[2,128,512]{1,2,0:T(8,128)(2,1)S(1)}, bf16[2,128,512]{1,2,0:T(8,128)(2,1)}, u32[]{:S(2)}) copy-start(bf16[2,128,512]{1,2,0:T(8,128)(2,1)} %copy.48) | copy-start | bytes 786436
  69.9 1.6 copy-start.2
  69.9 1.7 copy-start.9
  71.6 1.1 copy-start.5
  71.6 1.1 copy-start.10
  72.7 1.4 copy-start.6
  73.1 0.8 copy-start.3
  84.5 15.0 %copy-start.12 = (s32[2,32]{1,0:T(2,128)S(1)}, s32[2,32]{1,0:T(2,128)}, u32[]{:S(2)}) copy-start(s32[2,32]{1,0:T(2,128)} %param.11) | copy-start | bytes 772
  84.5 54.8 %all-to-all-start.2 = ((bf16[64,2,4,1536]{3,2,1,0:T(4,128)(2,1)}), bf16[64,2,4,1536]{3,2,1,0:T(4,128)(2,1)S(1)}, u32[]{:S(2)}, u32[]{:S(2)}) async-start(bf16[64,2,4,1536]{3,2,1,0:T(4,128)(2,1)} %bitcast.14), calls=%async_computation.2 | async-start | bytes 3145728 | tf_op jit(solution)/shard_map/all_to_all | solution.py:148
  139.3 15.3 %all-to-all-start.1 = ((s32[64,1,2]{2,1,0:T(1,128)}), s32[64,1,2]{2,1,0:T(1,128)S(1)}, u32[]{:S(2)}, u32[]{:S(2)}) async-start(s32[64,1,2]{2,1,0:T(1,128)} %bitcast.18), calls=%async_computation.1 | async-start | bytes 65536 | tf_op jit(solution)/shard_map/all_to_all | solution.py:150
  149.3 5.4 %copy-start.8 = (bf16[512,512]{0,1:T(8,128)(2,1)S(1)}, bf16[512,512]{0,1:T(8,128)(2,1)}, u32[]{:S(2)}) copy-start(bf16[512,512]{0,1:T(8,128)(2,1)} %copy.59) | copy-start | bytes 1572868
  175.6 26.5 %copy-start.4 = (f32[2,128,512]{2,1,0:T(8,128)S(1)}, f32[2,128,512]{2,1,0:T(8,128)}, u32[]{:S(2)}) copy-start(f32[2,128,512]{2,1,0:T(8,128)} %copy-done.3) | copy-start | bytes 1572868
  175.6 26.5 %copy-start.7 = (bf16[512,512]{1,0:T(8,128)(2,1)S(1)}, bf16[512,512]{1,0:T(8,128)(2,1)}, u32[]{:S(2)}) copy-start(bf16[512,512]{1,0:T(8,128)(2,1)} %param.17) | copy-start | bytes 1572868
  177.7 23.5 %all-to-all-start.3 = ((bf16[64,2,4,512]{3,2,1,0:T(4,128)(2,1)}), bf16[64,2,4,512]{3,2,1,0:T(4,128)(2,1)S(1)}, u32[]{:S(2)}, u32[]{:S(2)}) async-start(bf16[64,2,4,512]{3,2,1,0:T(4,128)(2,1)} %reshape_reshape.4), calls=%async_computation.3 | async-start | bytes 1048576 | tf_op jit(solution)/shard_map/all_to_all | solution.py:156
Sparse Core Ops, SparseCore 0:
  17.0 43.1 all-gather.1
where the time goes:
time: 211 us; the launch traced here: 210 us
  waiting for transfers between devices  87.1 us (41%)
  local copies, waits for them, and re-layouts  39.5 us (19%)
  starting transfers between devices  39 us (18%)
  matrix products  22 us (10%)
  between operations  13.7 us (6%)
  other arithmetic  7.28 us (3%)
    all_to_all x1, waiting for transfers between devices, on_device(): lax.all_to_all(packed(qkv_blocks, 0), 'wide', split_axis=0, concat_axis=0...  37.7 us
    all_gather x1, waiting for transfers between devices, on_device(): pooled_all = lax.all_gather(pooled, 'narrow', axis=1, tiled=True)  27.9 us
    all_to_all x1, waiting for transfers between devices, on_device(): lax.all_to_all(mixture.reshape(wide_count, capacity, BLK, model_width), '...  17.3 us
    all_to_all x1, starting transfers between devices, on_device(): lax.all_to_all(packed(qkv_blocks, 0), 'wide', split_axis=0, concat_axis=0...  15 us
    all_to_all x1, starting transfers between devices, on_device(): lax.all_to_all(ball_packed, 'wide', split_axis=0, concat_axis=0, tiled=True)  11.6 us
    slice x11, local copies, waits for them, and re-layouts, split_heads(): block_rows[..., offset:offset + model_width]  10.9 us
    scatter x3, local copies, waits for them, and re-layouts, packed(): return buffer.at[slot_of].set(block_data).reshape((wide_count, capacity)...  9.62 us
    sub x2, matrix products, one_block(): exponent = jnp.exp(scores - highest)  9.07 us
  transfers between devices with their start and end apart: 5, of which 4 were waited for; matrix products, arithmetic and copies ran while one was open for 14% of the time, Pallas kernels for 0%

commit v1 on v0

--- a/solution.py
+++ b/solution.py
@@ -115,7 +115,9 @@
     qkv_one = project(normed_one, qkv_first).astype(jnp.bfloat16)
     pooled = pool_rows(qkv_one, counts)
     usable = usable_points(counts)
-    pooled_all = lax.all_gather(pooled, "narrow", axis=1, tiled=True)
+    pooled_all = jnp.concatenate(
+        lax.all_to_all(jnp.stack([pooled] * lax.axis_size("narrow")), "narrow", 0, 0), axis=1
+    )
     attended_one = jax.vmap(fine_coarse)(qkv_one, usable, pooled_all)
     layer_one = (points.astype(jnp.float32) + project(attended_one, out_first)).astype(jnp.bfloat16)
     normed_two = rms_round(layer_one)

time: 211 us -> 199 us (0.943)
  between operations: 13.7 us -> 0.33 us
  waiting for transfers between devices: 87.1 us -> 79.9 us
  starting transfers between devices: 39 us -> 44.3 us
  local copies, waits for them, and re-layouts: 39.5 us -> 41.7 us
    all_gather x1 -> x0, waiting for transfers between devices: 27.9 us -> none  [on_device(): pooled_all = lax.all_gather(pooled, 'narrow', axis=1, tiled=True)]
    all_to_all x0 -> x1, waiting for transfers between devices: none -> 20.7 us  [on_device(): lax.all_to_all(jnp.stack([pooled] * lax.axis_size('narrow')), 'narrow', 0...]
    all_to_all x0 -> x1, starting transfers between devices: none -> 10.9 us  [on_device(): lax.all_to_all(jnp.stack([pooled] * lax.axis_size('narrow')), 'narrow', 0...]
    all_to_all x1, starting transfers between devices: 15 us -> 10.5 us  [on_device(): lax.all_to_all(packed(qkv_blocks, 0), 'wide', split_axis=0, concat_axis=0...]
  transfers between devices with their start and end apart: 5 -> 5, of which waited for: 4 -> 4; matrix products, arithmetic and copies ran while one was open for 14% -> 17% of each run, Pallas kernels for 0% -> 0%
where the time goes in v1:
time: 199 us; the launch traced here: 198 us
  waiting for transfers between devices  79.9 us (40%)
  starting transfers between devices  44.3 us (22%)
  local copies, waits for them, and re-layouts  41.7 us (21%)
  matrix products  23 us (12%)
  other arithmetic  7.28 us (4%)
    all_to_all x1, waiting for transfers between devices, on_device(): lax.all_to_all(packed(qkv_blocks, 0), 'wide', split_axis=0, concat_axis=0...  37.7 us
    all_to_all x1, waiting for transfers between devices, on_device(): lax.all_to_all(jnp.stack([pooled] * lax.axis_size('narrow')), 'narrow', 0...  20.7 us
    all_to_all x1, waiting for transfers between devices, on_device(): lax.all_to_all(mixture.reshape(wide_count, capacity, BLK, model_width), '...  17.3 us
    slice x11, local copies, waits for them, and re-layouts, split_heads(): block_rows[..., offset:offset + model_width]  12.7 us
    all_to_all x1, starting transfers between devices, on_device(): lax.all_to_all(jnp.stack([pooled] * lax.axis_size('narrow')), 'narrow', 0...  10.9 us
    all_to_all x1, starting transfers between devices, on_device(): lax.all_to_all(ball_packed, 'wide', split_axis=0, concat_axis=0, tiled=True)  10.6 us
    all_to_all x1, starting transfers between devices, on_device(): lax.all_to_all(packed(qkv_blocks, 0), 'wide', split_axis=0, concat_axis=0...  10.5 us
    scatter x3, local copies, waits for them, and re-layouts, packed(): return buffer.at[slot_of].set(block_data).reshape((wide_count, capacity)...  9.62 us
  transfers between devices with their start and end apart: 5, of which 4 were waited for; matrix products, arithmetic and copies ran while one was open for 17% of the time, Pallas kernels for 0%

profile of v1, /device:TPU:1, one launch (start us, length us, event | category | flops | bytes accessed | tf_op | source)
XLA Modules:
  0.0 197.8 jit_solution(924362978525560788)
XLA Ops:
  0.0 1.2 fusion.35
  1.2 0.7 convert_element_type.90
  1.9 0.7 lt.53
  2.9 1.6 convolution_convert_fusion.1
  4.5 1.1 convert_multiply_fusion
  5.6 1.5 reshape.251
  7.1 1.4 reduce_sum.66
  8.5 1.0 divide_convert_fusion.8
  9.5 1.1 stack.2
  10.6 10.9 %all-to-all-start = ((bf16[8,2,32,1024]{3,2,1,0:T(8,128)(2,1)}), bf16[8,2,32,1024]{3,2,1,0:T(8,128)(2,1)S(1)}, u32[]{:S(2)}, u32[]{:S(2)}) async-start(bf16[8,2,32,1024]{3,2,1,0:T(8,128)(2,1)} %stack.2), calls=%async_computation | async-start | bytes 2097152 | tf_op jit(solution)/shard_map/all_to_all | solution.py:119
  21.5 0.9 fusion.58
  22.4 1.1 copy.53
  23.6 1.1 copy.54
  24.7 1.8 copy.52
  26.9 0.2 select_reduce_fusion
  27.1 0.8 scatter_custom_fusion
  27.9 0.7 all_to_all.22
  28.6 1.3 fusion.59
  30.0 20.7 %all-to-all-done = bf16[8,2,32,1024]{3,2,1,0:T(8,128)(2,1)S(1)} async-done(((bf16[8,2,32,1024]{3,2,1,0:T(8,128)(2,1)}), bf16[8,2,32,1024]{3,2,1,0:T(8,128)(2,1)S(1)}, u32[]{:S(2)}, u32[]{:S(2)}) %all-to-all-start) | async-done | bytes 1048608 | tf_op jit(solution)/shard_map/all_to_all | solution.py:119
  50.7 10.6 %all-to-all-start.1 = ((s32[64,1,2]{2,1,0:T(1,128)}), s32[64,1,2]{2,1,0:T(1,128)S(1)}, u32[]{:S(2)}, u32[]{:S(2)}) async-start(s32[64,1,2]{2,1,0:T(1,128)} %bitcast.14), calls=%async_computation.1 | async-start | bytes 65536 | tf_op jit(solution)/shard_map/all_to_all | solution.py:151
  61.4 0.9 fusion.57
  62.3 2.1 %copy.56 = bf16[2,256,512]{1,2,0:T(8,128)(2,1)} copy(bf16[2,256,512]{2,1,0:T(8,128)(2,1)} %get-tuple-element.129) | data formatting | bytes 1048576 | tf_op jit(solution)/shard_map/vmap()/slice | solution.py:27
  64.5 1.6 multiply_reduce_fusion
  66.1 0.2 fusion.34
  66.3 1.1 copy-done.1
  67.4 0.7 fusion.26
  68.2 1.0 copy.58
  69.2 0.3 fusion.39
  69.5 1.3 copy-done.2
  70.8 1.1 fusion.30
  72.0 0.4 multiply_reduce_fusion.1
  72.4 0.8 copy-done.3
  73.2 0.2 copy-done.7
  73.3 0.6 convolution_convert_fusion
  73.9 0.2 reshape.294
  74.1 1.6 broadcast_in_dim.71
  75.7 8.1 %scatter_fusion = bf16[128,4,1536]{2,1,0:T(4,128)(2,1)} fusion(bf16[128,4,1536]{2,1,0:T(4,128)(2,1)} %broadcast_in_dim.71, s32[64]{0:T(128)S(1)} %fusion.44, bf16[64,4,1536]{2,1,0:T(4,128)(2,1)S(1)} %reshape.294), kind=kCustom, calls=%fused_computation.3 | custom fusion | bytes 2359552 | tf_op jit(solution)/shard_map/scatter | solution.py:141
  83.8 10.5 %all-to-all-start.3 = ((bf16[64,2,4,1536]{3,2,1,0:T(4,128)(2,1)}), bf16[64,2,4,1536]{3,2,1,0:T(4,128)(2,1)S(1)}, u32[]{:S(2)}, u32[]{:S(2)}) async-start(bf16[64,2,4,1536]{3,2,1,0:T(4,128)(2,1)} %bitcast.17), calls=%async_computation.3 | async-start | bytes 3145728 | tf_op jit(solution)/shard_map/all_to_all | solution.py:150
  94.3 0.8 scatter_custom_fusion.1
  95.1 0.8 all_to_all.24
  96.3 37.7 %all-to-all-done.3 = bf16[64,2,4,1536]{3,2,1,0:T(4,128)(2,1)S(1)} async-done(((bf16[64,2,4,1536]{3,2,1,0:T(4,128)(2,1)}), bf16[64,2,4,1536]{3,2,1,0:T(4,128)(2,1)S(1)}, u32[]{:S(2)}, u32[]{:S(2)}) %all-to-all-start.3) | async-done | bytes 1572896 | tf_op jit(solution)/shard_map/all_to_all | solution.py:150
  134.0 6.1 %all-to-all-start.2 = ((s32[64,1,2]{2,1,0:T(1,128)}), s32[64,1,2]{2,1,0:T(1,128)S(1)}, u32[]{:S(2)}, u32[]{:S(2)}) async-start(s32[64,1,2]{2,1,0:T(1,128)} %bitcast.21), calls=%async_computation.2 | async-start | bytes 65536 | tf_op jit(solution)/shard_map/all_to_all | solution.py:152
  140.2 1.4 reshape.261
  141.5 1.5 fusion.56
  143.0 1.0 copy.63
  144.0 1.0 copy.64
  145.0 0.2 copy.65
  145.2 4.1 %all-to-all-done.2 = s32[64,1,2]{2,1,0:T(1,128)S(1)} async-done(((s32[64,1,2]{2,1,0:T(1,128)}), s32[64,1,2]{2,1,0:T(1,128)S(1)}, u32[]{:S(2)}, u32[]{:S(2)}) %all-to-all-start.2) | async-done | bytes 544 | tf_op jit(solution)/shard_map/all_to_all | solution.py:152
  149.4 20.9 %while.11 = (s32[]{:T(128)}, bf16[2,256,512]{2,1,0:T(8,128)(2,1)}, s32[2]{0:T(128)S(1)}, s32[512]{0:T(512)S(1)}, bf16[512,8,64]{0,2,1:T(8,128)(2,1)S(1)}, /*inde...) while((s32[]{:T(128)}, bf16[2,256,512]{2,1,0:T(8,128)(2,1)}, ...), condition=%wide.region_15.16_spmd.clone, body=%wide.region_12.15_spmd.clone.sunk | while | flops 275121152 | bytes 11303615 | solution.py:106
  149.4 0.6 dynamic_slice.29
  151.2 0.2 compare_and_fusion.2
  151.4 4.5 %fusion.79 = (f32[8,256]{1,0:T(8,128)S(1)}, f32[8,256,512]{2,1,0:T(8,128)}) fusion(pred[256,512]{1,0:T(8,128)(4,1)S(1)} %compare_and_fusion.2, bf16[512,8,64]{0,2,1:T(8,128)(2,1)} %get-tuple-element.229, bf16[512,8,64]{0,2,1:T(8,128)(2,1)S(1)} %get-tuple-element.228, s32[]{:T(128)S(6)} %select_n.46), kind=kOutput, calls=%fused_computation.77.clone.1 | convolution fusion | flops 138412544 | bytes 5120004 | tf_op jit(solution)/shard_map/while/body/eval_jaxpr/sub | solution.py:99
  155.9 3.0 %fusion.80 = bf16[8,256,64]{1,2,0:T(8,128)(2,1)S(1)} fusion(bf16[512,8,64]{0,2,1:T(8,128)(2,1)S(1)} %get-tuple-element.230, f32[8,256,512]{2,1,0:T(8,128)} %get-tuple-element.196, f32[8,256]{1,0:T(8,128)S(1)} %get-tuple-element.197), kind=kOutput, calls=%fused_computation.15.clone.1 | convolution fusion | flops 136445952 | bytes 4988928 | tf_op jit(solution)/shard_map/while/body/eval_jaxpr/hqk,khe->qhe/dot_general | solution.py:101
  159.1 0.7 constant_dynamic-update-slice_fusion.2
  159.8 0.6 dynamic_slice.29
  161.7 0.2 compare_and_fusion.2
  161.9 4.5 %fusion.79 = (f32[8,256]{1,0:T(8,128)S(1)}, f32[8,256,512]{2,1,0:T(8,128)}) fusion(pred[256,512]{1,0:T(8,128)(4,1)S(1)} %compare_and_fusion.2, bf16[512,8,64]{0,2,1:T(8,128)(2,1)} %get-tuple-element.229, bf16[512,8,64]{0,2,1:T(8,128)(2,1)S(1)} %get-tuple-element.228, s32[]{:T(128)S(6)} %select_n.46), kind=kOutput, calls=%fused_computation.77.clone.1 | convolution fusion | flops 138412544 | bytes 5120004 | tf_op jit(solution)/shard_map/while/body/eval_jaxpr/sub | solution.py:99
  166.4 3.0 %fusion.80 = bf16[8,256,64]{1,2,0:T(8,128)(2,1)S(1)} fusion(bf16[512,8,64]{0,2,1:T(8,128)(2,1)S(1)} %get-tuple-element.230, f32[8,256,512]{2,1,0:T(8,128)} %get-tuple-element.196, f32[8,256]{1,0:T(8,128)S(1)} %get-tuple-element.197), kind=kOutput, calls=%fused_computation.15.clone.1 | convolution fusion | flops 136445952 | bytes 4988928 | tf_op jit(solution)/shard_map/while/body/eval_jaxpr/hqk,khe->qhe/dot_general | solution.py:101
  169.6 0.7 constant_dynamic-update-slice_fusion.2
  170.3 2.1 %reshape_reshape.4 = bf16[64,2,4,512]{3,2,1,0:T(4,128)(2,1)} reshape(bf16[2,256,512]{2,1,0:T(8,128)(2,1)} %get-tuple-element.52) | data formatting | bytes 1048576 | tf_op jit(solution)/shard_map/reshape;reshape | solution.py:159
  172.4 6.2 %all-to-all-start.4 = ((bf16[64,2,4,512]{3,2,1,0:T(4,128)(2,1)}), bf16[64,2,4,512]{3,2,1,0:T(4,128)(2,1)S(1)}, u32[]{:S(2)}, u32[]{:S(2)}) async-start(bf16[64,2,4,512]{3,2,1,0:T(4,128)(2,1)} %reshape_reshape.4), calls=%async_computation.4 | async-start | bytes 1048576 | tf_op jit(solution)/shard_map/all_to_all | solution.py:158
  178.6 17.3 %all-to-all-done.4 = bf16[64,2,4,512]{3,2,1,0:T(4,128)(2,1)S(1)} async-done(((bf16[64,2,4,512]{3,2,1,0:T(4,128)(2,1)}), bf16[64,2,4,512]{3,2,1,0:T(4,128)(2,1)S(1)}, u32[]{:S(2)}, u32[]{:S(2)}) %all-to-all-start.4) | async-done | bytes 524320 | tf_op jit(solution)/shard_map/all_to_all | solution.py:158
  195.9 0.8 gather_fusion
  196.8 1.0 fusion.33
  (66 shorter events, 3.0 us)
Async XLA Ops:
  0.0 2.9 %copy-start = (bf16[512,1536]{1,0:T(8,128)(2,1)S(1)}, bf16[512,1536]{1,0:T(8,128)(2,1)}, u32[]{:S(2)}) copy-start(bf16[512,1536]{1,0:T(8,128)(2,1)} %param.14) | copy-start | bytes 4718596
  10.6 40.1 %all-to-all-start = ((bf16[8,2,32,1024]{3,2,1,0:T(8,128)(2,1)}), bf16[8,2,32,1024]{3,2,1,0:T(8,128)(2,1)S(1)}, u32[]{:S(2)}, u32[]{:S(2)}) async-start(bf16[8,2,32,1024]{3,2,1,0:T(8,128)(2,1)} %stack.2), calls=%async_computation | async-start | bytes 2097152 | tf_op jit(solution)/shard_map/all_to_all | solution.py:119
  21.5 5.0 %copy-start.14 = (s32[2,32]{1,0:T(2,128)S(1)}, s32[2,32]{1,0:T(2,128)}, u32[]{:S(2)}) copy-start(s32[2,32]{1,0:T(2,128)} %param.12) | copy-start | bytes 772
  21.5 5.1 %copy-start.15 = (s32[2,32]{1,0:T(2,128)S(1)}, s32[2,32]{1,0:T(2,128)}, u32[]{:S(2)}) copy-start(s32[2,32]{1,0:T(2,128)} %param.13) | copy-start | bytes 772
  50.7 33.1 %all-to-all-start.1 = ((s32[64,1,2]{2,1,0:T(1,128)}), s32[64,1,2]{2,1,0:T(1,128)S(1)}, u32[]{:S(2)}, u32[]{:S(2)}) async-start(s32[64,1,2]{2,1,0:T(1,128)} %bitcast.14), calls=%async_computation.1 | async-start | bytes 65536 | tf_op jit(solution)/shard_map/all_to_all | solution.py:151
  62.3 3.8 %copy-start.5 = (f32[2,8,128,128]{2,3,1,0:T(8,128)S(1)}, f32[2,8,128,128]{2,3,1,0:T(8,128)}, u32[]{:S(2)}) copy-start(f32[2,8,128,128]{2,3,1,0:T(8,128)} %get-tuple-element.134) | copy-start | bytes 3145732
  66.1 1.4 copy-start.1
  66.1 3.1 %copy-start.12 = (bf16[2,128,512]{1,2,0:T(8,128)(2,1)S(1)}, bf16[2,128,512]{1,2,0:T(8,128)(2,1)}, u32[]{:S(2)}) copy-start(bf16[2,128,512]{1,2,0:T(8,128)(2,1)} %copy.52) | copy-start | bytes 786436
  69.2 1.6 copy-start.2
  69.2 1.7 copy-start.10
  70.8 1.1 copy-start.6
  70.8 1.1 copy-start.11
  71.9 1.4 copy-start.7
  72.4 0.8 copy-start.3
  83.8 10.5 %copy-start.13 = (s32[2,32]{1,0:T(2,128)S(1)}, s32[2,32]{1,0:T(2,128)}, u32[]{:S(2)}) copy-start(s32[2,32]{1,0:T(2,128)} %param.11) | copy-start | bytes 772
  83.8 50.3 %all-to-all-start.3 = ((bf16[64,2,4,1536]{3,2,1,0:T(4,128)(2,1)}), bf16[64,2,4,1536]{3,2,1,0:T(4,128)(2,1)S(1)}, u32[]{:S(2)}, u32[]{:S(2)}) async-start(bf16[64,2,4,1536]{3,2,1,0:T(4,128)(2,1)} %bitcast.17), calls=%async_computation.3 | async-start | bytes 3145728 | tf_op jit(solution)/shard_map/all_to_all | solution.py:150
  134.0 15.3 %all-to-all-start.2 = ((s32[64,1,2]{2,1,0:T(1,128)}), s32[64,1,2]{2,1,0:T(1,128)S(1)}, u32[]{:S(2)}, u32[]{:S(2)}) async-start(s32[64,1,2]{2,1,0:T(1,128)} %bitcast.21), calls=%async_computation.2 | async-start | bytes 65536 | tf_op jit(solution)/shard_map/all_to_all | solution.py:152
  144.0 5.4 %copy-start.9 = (bf16[512,512]{0,1:T(8,128)(2,1)S(1)}, bf16[512,512]{0,1:T(8,128)(2,1)}, u32[]{:S(2)}) copy-start(bf16[512,512]{0,1:T(8,128)(2,1)} %copy.63) | copy-start | bytes 1572868
  170.3 26.5 %copy-start.4 = (f32[2,128,512]{2,1,0:T(8,128)S(1)}, f32[2,128,512]{2,1,0:T(8,128)}, u32[]{:S(2)}) copy-start(f32[2,128,512]{2,1,0:T(8,128)} %copy-done.3) | copy-start | bytes 1572868
  170.3 26.5 %copy-start.8 = (bf16[512,512]{1,0:T(8,128)(2,1)S(1)}, bf16[512,512]{1,0:T(8,128)(2,1)}, u32[]{:S(2)}) copy-start(bf16[512,512]{1,0:T(8,128)(2,1)} %param.17) | copy-start | bytes 1572868
  172.4 23.5 %all-to-all-start.4 = ((bf16[64,2,4,512]{3,2,1,0:T(4,128)(2,1)}), bf16[64,2,4,512]{3,2,1,0:T(4,128)(2,1)S(1)}, u32[]{:S(2)}, u32[]{:S(2)}) async-start(bf16[64,2,4,512]{3,2,1,0:T(4,128)(2,1)} %reshape_reshape.4), calls=%async_computation.4 | async-start | bytes 1048576 | tf_op jit(solution)/shard_map/all_to_all | solution.py:158
